TPU v7x, 128 devices: a whole 4x4x4 slice. The times are simulated.
128 devices in a mesh: gx: 8 (over x, core), gy: 16 (over z, y).
Axes of the slice: x: 4, y: 4, z: 4, core: 2. Of those that a mesh axis runs over, the one named last changes fastest.
Arguments:
- potential_heat: float32 [3, 384, 12288], P(None, 'gx', 'gy'), may hold values from -6 to 6
- easterly_speed: float32 [3, 384, 12288], P(None, 'gx', 'gy'), may hold values from -6 to 6
- poleward_speed: float32 [3, 384, 12288], P(None, 'gx', 'gy'), may hold values from -6 to 6
- sea_elevation: float32 [384, 12288], P('gx', 'gy'), may hold values from -6 to 6
- averaged_easterly_speed: float32 [384, 12288], P('gx', 'gy'), may hold values from -6 to 6
- averaged_poleward_speed: float32 [384, 12288], P('gx', 'gy'), may hold values from -6 to 6
- seafloor_distance: float32 [384, 12288], P('gx', 'gy'), may hold values from 0.5 to 2
- marine_indicator: int32 [384, 12288], P('gx', 'gy'), may hold values from 0 to 1, as said below
- hilbert_tile_sequence: int32 [1024], replicated, may hold values from -1 to 2047, as said below
Outputs:
- temp_next: float32 [3, 48, 49152], P(None, None, ('gx', 'gy'))
- zonal_next: float32 [3, 48, 49152], P(None, None, ('gx', 'gy'))
- merid_next: float32 [3, 48, 49152], P(None, None, ('gx', 'gy'))
- surface_next: float32 [48, 49152], P(None, ('gx', 'gy'))
- east_next: float32 [48, 49152], P(None, ('gx', 'gy'))
- north_next: float32 [48, 49152], P(None, ('gx', 'gy'))
Inputs may be any that keep to these rules, and one draw needn't show every extreme that they name: Slot s = (device index times 8) plus slot, with device index = gx index times the size of gy plus gy index, holds block hilbert_tile_sequence[s] = latitude row times 256 plus longitude column, or -1 if empty. Every block that hilbert_tile_sequence lists appears exactly once. A device's blocks all lie in the latitude row equal to its gx index, fill its first slots, and number at least one and at most 8; some device holds 8. `marine_indicator`: zero throughout every block that hilbert_tile_sequence does not list.
All inputs are finite; a program needn't handle non-finite values.
Results may differ from a plain program's by a relative error of at most 0.0003.
Values sent between devices are 32-bit elements; how exact they have to be, the bound alone decides.
No kernel may reach another device: no remote copies, remote signals or barrier semaphores. Data moves between devices by JAX's collectives and lax.ppermute only.
A program may use at most 128 MiB of HBM per device.

v0:
```python
import functools

import jax
import jax.numpy as jnp
from jax import lax
from jax.experimental import pallas as pl
from jax.experimental.pallas import tpu as pltpu
from jax.sharding import PartitionSpec as P

BLOCK = 48
SLOTS = 8
ROW_DEVICES = 16
GRID_ROWS = 8
LAT = 384
PLANES = 14
WET = 13
LANES = 128
PIECE = 112

F32 = jnp.float32
I32 = jnp.int32


def iota(shape, dim):
    return lax.broadcasted_iota(I32, shape, dim)


def roll(x, shift, axis):
    return pltpu.roll(x, shift % x.shape[axis], axis)


def plane_of(refs, p):
    if p < 9:
        return refs[p // 3], (p % 3,)
    return refs[3 + p - 9], ()


def read_plane(refs, p, rows, lanes):
    ref, lead = plane_of(refs, p)
    x = ref[lead + (rows, lanes)]
    return x.astype(F32) if p == WET else x


def halo_tile(north, south, p):
    low = iota(north.shape, 0) < 4
    if p < 7:
        return jnp.where(low, north, roll(south, 4, 0))
    return jnp.where(low, roll(north, 4, 0), south)


def edge_kernel(*refs):
    raw = refs[:8]
    row_a, row_b = refs[8:10]
    parts, sem = refs[10:26], refs[26]
    copies = []
    for i, rows in enumerate((slice(0, 8), slice(40, 48))):
        for j, x in enumerate(raw):
            where = (slice(None),) * (len(x.shape) - 2) + (rows, slice(None))
            n = 8 * i + j
            copies.append(pltpu.make_async_copy(x.at[where], parts[n], sem.at[n]))
            copies[-1].start()
    for copy in copies:
        copy.wait()
    bottoms, tops = parts[:8], parts[8:]
    even = lax.axis_index("gx") % 2 == 0
    low = iota((8, 768), 0) < 4
    full = slice(None)
    for m in range(7):
        t0, t1 = (read_plane(tops, q, full, full) for q in (m, m + 7))
        b0, b1 = (read_plane(bottoms, q, full, full) for q in (m, m + 7))
        top = jnp.where(low, roll(t0, 4, 0), t1)
        bottom = jnp.where(low, b0, roll(b1, 4, 0))
        row_a[8 * m : 8 * m + 8] = jnp.where(even, top, bottom)
        row_b[8 * m : 8 * m + 8] = jnp.where(even, bottom, top)


def place_tables(tab_ref, idx, full):
    gx, gy = lax.axis_index("gx"), lax.axis_index("gy")
    square = (LANES, LANES)
    g = tab_ref[pl.ds(gx, 1), :].astype(F32)
    g_lane = jnp.broadcast_to(g, square)
    diagonal = iota(square, 0) == iota(square, 1)
    g_sub = jnp.sum(jnp.where(diagonal, g_lane, 0.0), axis=1, keepdims=True)
    g_sub = jnp.broadcast_to(g_sub, square)
    d_lane = jnp.floor(g_lane * (1.0 / 16.0))
    d_sub = jnp.floor(g_sub * (1.0 / 16.0))
    same = d_lane == d_sub
    rank_lane = jnp.sum(jnp.where(same & (g_sub < g_lane), 1.0, 0.0), axis=0, keepdims=True)
    rank_sub = jnp.sum(jnp.where(same & (g_lane < g_sub), 1.0, 0.0), axis=1, keepdims=True)
    first = (gx * ROW_DEVICES).astype(F32)
    source = jnp.floor(g * (1.0 / 16.0)) - first
    listed = g >= 0.0
    half = jnp.where(rank_lane >= 8.0, 1.0, 0.0)
    half = jnp.where(listed, half, 0.0)
    place = jnp.where(listed, source, 0.0)
    off = jnp.where(listed, 48.0 * (rank_lane - 8.0 * half), 0.0)
    tile = jnp.floor(off * (1.0 / LANES))
    own = (iota((1, LANES), 1) // SLOTS == gy) & listed
    used = jnp.sum(jnp.where(own, float(BLOCK), 0.0), axis=1, keepdims=True)
    used = jnp.broadcast_to(used, (1, LANES))
    me = (gx * ROW_DEVICES + gy).astype(F32)
    c_lane = iota(square, 1).astype(F32)
    mine = (d_sub == me) & (jnp.broadcast_to(rank_sub, square) == c_lane)
    order = jnp.sum(jnp.where(mine, g_sub - d_sub * 16.0, 0.0), axis=0, keepdims=True)
    count = jnp.zeros(square, F32)
    for r in range(GRID_ROWS):
        owner = jnp.floor(tab_ref[r : r + 1, :].astype(F32) * (1.0 / 16.0))
        count += jnp.where(jnp.broadcast_to(owner, square) == iota(square, 0).astype(F32), 1.0, 0.0)
    most = jnp.max(jnp.sum(count, axis=1, keepdims=True), axis=0, keepdims=True)
    most = jnp.broadcast_to(most, (1, LANES))
    sub = iota((8, LANES), 0)
    table = jnp.where(sub == 3, order, most)
    table = jnp.where(sub == 0, place * PIECE + 36.0 * tile, table)
    table = jnp.where(sub == 1, place * PIECE + 36.0 * jnp.minimum(tile + 1.0, 2.0), table)
    table = jnp.where(sub == 2, off - LANES * tile, table)
    table = jnp.where(sub == 5, used, table)
    table = jnp.where(sub == 6, half, table)
    idx[...] = table.astype(I32)
    full[...] = most[:, :1].astype(I32)


def column_kernel(row_a, row_b, col_e, col_w, col_a, col_b):
    gx, gy = lax.axis_index("gx"), lax.axis_index("gy")
    even_row, even = gx % 2 == 0, gy % 2 == 0
    lane = iota((8, LANES), 1)
    east = jnp.zeros((8, LANES), F32)
    west = jnp.zeros((8, LANES), F32)
    for p in range(PLANES):
        rows = slice(8 * (p % 7), 8 * (p % 7) + 8)
        here = (lane >= 4 * p) & (lane < 4 * p + 4)
        w, e = (
            halo_tile(jnp.where(even_row, a, b), jnp.where(even_row, b, a), p)
            for a, b in (
                (row_a[rows, i : i + LANES], row_b[rows, i : i + LANES]) for i in (0, 640)
            )
        )
        east = jnp.where(here, roll(e, 4 * p + 4, 1), east)
        west = jnp.where(here, roll(w, 4 * p, 1), west)
    e_own, w_own = col_e[...], col_w[...]
    col_a[0:48] = jnp.where(even, e_own, w_own)
    col_b[0:48] = jnp.where(even, w_own, e_own)
    col_a[48:56] = jnp.where(even, east, west)
    col_b[48:56] = jnp.where(even, west, east)


HT = 56
STRIP = 72
STRIPS = 7
T0, U0, V0 = 0, 3, 6
XE, XW, YN, YS = 9, 12, 15, 18
E0, P0, Q0, DEPTH, WETS, QUARTER, DP, DQ, GX, GY = range(21, 31)
FIELDS = 31


def pack_tiles(r):
    lane = iota(r[0].shape, 1)
    t0 = jnp.where(lane < 48, r[0], jnp.where(lane < 96, r[1], r[2]))
    t1 = jnp.where(
        lane < 16, r[2], jnp.where(lane < 64, r[3], jnp.where(lane < 112, r[4], r[5]))
    )
    t2 = jnp.where(lane < 32, r[5], jnp.where(lane < 80, r[6], r[7]))
    return t0, t1, t2


class Step:
    def __init__(self, ext, res):
        self.ext, self.res = ext, res
        self.gx, self.gy = lax.axis_index("gx"), lax.axis_index("gy")

    def put(self, field, t, x, first=8):
        self.ext[field, t, first : first + x.shape[0]] = x

    def mid(self, field, t, first=8, rows=HT):
        return self.ext[field, t, first : first + rows]

    def right(self, field, t, x, k=1, first=8):
        after = t if isinstance(t, int) and t in (5, 6) else t + 1
        lane = iota(x.shape, 1)
        y = self.mid(field, after, first, x.shape[0])
        return roll(jnp.where(lane < k, y, x), -k, 1)

    def left(self, field, t, x, k=1, first=8):
        before = t if isinstance(t, int) and t in (0, 6) else t - 1
        lane = iota(x.shape, 1)
        y = self.mid(field, before, first, x.shape[0])
        return roll(jnp.where(lane >= LANES - k, y, x), k, 1)

    def place(self, t, planes, part):
        def put(field, x, ring=False):
            if part == "halo":
                self.put(field, t, x, 56)
                if ring:
                    self.put(field, t, x, 0)
            else:
                self.put(field, t, x)
                if ring:
                    self.put(field, t, x[0:8], 64)
                    if part == "all":
                        self.put(field, t, x[48:56], 0)

        wet = planes(WET)
        put(WETS, wet)
        put(QUARTER, 0.25 * wet)
        sums = []
        for q in range(3):
            heat = planes(q) * wet
            put(T0 + q, heat, ring=True)
            b = heat - 0.1 * heat * heat
            sums.append(sums[-1] + b if sums else b)
        mean = (sums[0] + sums[1] + sums[2]) * (1.0 / 3.0)
        for q in range(3):
            push = 0.15 * (sums[q] - mean)
            u, v = planes(3 + q) * wet, planes(6 + q) * wet
            put(U0 + q, u, ring=True)
            put(V0 + q, v)
            u, v = 0.1 * u, 0.1 * v
            put(XE + q, u - push)
            put(XW + q, u + push)
            put(YN + q, v - push, ring=True)
            put(YS + q, v + push, ring=True)
        put(E0, planes(9) * wet)
        east, north = planes(10) * wet, planes(11) * wet
        depth = 0.25 * planes(12)
        put(P0, east)
        put(Q0, north)
        put(DEPTH, depth)
        put(DP, depth * east)
        put(DQ, depth * north, ring=True)

    def tracer(self, t, first, rows):
        mid = functools.partial(self.mid, t=t, rows=rows)
        wet = mid(WETS, first=first)
        for q in range(3):
            f = T0 + q
            x = mid(f, first=first)
            xe, xw = self.right(f, t, x, 1, first), self.left(f, t, x, 1, first)
            xee, xww = self.right(f, t, x, 2, first), self.left(f, t, x, 2, first)
            xn, xs = mid(f, first=first + 1), mid(f, first=first - 1)
            xnn, xss = mid(f, first=first + 2), mid(f, first=first - 2)
            dx = (3.2 / 12.0) * (xw - xe) + (0.4 / 12.0) * (xee - xww)
            dy = (3.2 / 12.0) * (xs - xn) + (0.4 / 12.0) * (xnn - xss)
            ring = 0.1 * ((xe + xw) + (xn + xs))
            u, v = mid(U0 + q, first=first), mid(V0 + q, first=first)
            new = 0.6 * x + ring + (u * dx + v * dy)
            self.res[t, 48 * q + first - 8 : 48 * q + first - 8 + rows] = wet * new

    def motion(self, t, first, rows):
        row = iota((rows, LANES), 0) + (first - 8)
        north = self.gx * BLOCK + row - jnp.where(row >= 52, HT, 0)
        turn = 0.15 * (2.0 * (north.astype(F32) + 0.5) / LAT - 1.0)
        mid = functools.partial(self.mid, t=t, rows=rows)
        wet = mid(WETS, first=first)
        kept = min(rows, 56 - first)
        gain_x = gain_y = None
        for q in range(3):
            u, v = mid(U0 + q, first=first), mid(V0 + q, first=first)
            xe, xw = mid(XE + q, first=first), mid(XW + q, first=first)
            side_x = self.right(XE + q, t, xe, 1, first) + self.left(XW + q, t, xw, 1, first)
            side_y = mid(YN + q, first=first + 1) + mid(YS + q, first=first - 1)
            ring_u = 0.1 * (mid(U0 + q, first=first + 1) + mid(U0 + q, first=first - 1))
            ring_v = 0.1 * (
                self.right(V0 + q, t, v, 1, first) + self.left(V0 + q, t, v, 1, first)
            )
            new_u = wet * ((0.6 * u + turn * v) + (side_x + ring_u))
            new_v = wet * ((0.6 * v - turn * u) + (side_y + ring_v))
            spot = 144 + 48 * q + first - 8
            self.res[t, spot : spot + kept] = new_u[:kept]
            self.res[t, spot + 144 : spot + 144 + kept] = new_v[:kept]
            du, dv = new_u - u, new_v - v
            gain_x = du if gain_x is None else gain_x + du
            gain_y = dv if gain_y is None else gain_y + dv
        self.put(GX, t, gain_x * (1.0 / 3.0), first)
        self.put(GY, t, gain_y * (1.0 / 3.0), first)

    def passes(self, strips):
        mid, put = self.mid, self.put
        for last in (False, True):
            for t in strips:
                flux = mid(DP, t)
                div = (self.right(DP, t, flux) - self.left(DP, t, flux)) + (
                    mid(DQ, t, 9) - mid(DQ, t, 7)
                )
                new = mid(E0, t) - mid(WETS, t) * div
                put(E0, t, new)
                put(E0, t, new[48:56], 0)
                put(E0, t, new[0:8], 64)
                if last:
                    self.res[t, 432:480] = new[:48]
            for t in strips:
                e, quarter = mid(E0, t), mid(QUARTER, t)
                ex = self.right(E0, t, e) - self.left(E0, t, e)
                ey = mid(E0, t, 9) - mid(E0, t, 7)
                new_p = (mid(P0, t) + mid(GX, t)) - quarter * ex
                new_q = (mid(Q0, t) + mid(GY, t)) - quarter * ey
                if last:
                    self.res[t, 480:528] = new_p[:48]
                    self.res[t, 528:576] = new_q[:48]
                else:
                    cross = mid(DEPTH, t) * new_q
                    put(P0, t, new_p)
                    put(Q0, t, new_q)
                    put(DP, t, mid(DEPTH, t) * new_p)
                    put(DQ, t, cross)
                    put(DQ, t, cross[48:56], 0)
                    put(DQ, t, cross[0:8], 64)


def cut_pieces(rounds, idx, res, send):
    spots = []
    for c in range(8 * rounds):
        off = 48 * idx[3, c]
        inner = off & 127
        spots.append((off >> 7, inner, (48 * c + 256 - inner) & 127))

    def cut(q):
        pair = 2 * q
        for h in range(rounds):
            done = []
            for start, n in ((64 * q, 64), (512 + 8 * q, 8)):
                rows = pl.ds(start, n) if isinstance(q, int) else pl.ds(pl.multiple_of(start, 8), n)
                lanes = iota((n, LANES), 1)
                moved = []
                for tile, inner, shift in spots[8 * h : 8 * h + 8]:
                    x = jnp.where(lanes >= inner, res[tile, rows], res[tile + 1, rows])
                    moved.append(pltpu.roll(x, shift, 1))
                done.append(pack_tiles(moved))
            mains, rests = done
            for i in range(3):
                base = PIECE * h + 36 * i
                send[pair, base + 32 : base + 40] = rests[i]
                send[pair + 1, base + 28 : base + 36] = rests[i]
            for i in range(3):
                base = PIECE * h + 36 * i
                send[pair, base : base + 32] = mains[i][:32]
                send[pair + 1, base : base + 32] = mains[i][32:]

    if rounds == 1:
        for q in range(8):
            cut(q)
    else:
        pl.loop(0, 8)(cut)


def interior_kernel(*refs):
    tab, raw = refs[0], refs[2:10]
    ext, res, idx, most, edge, col_e, col_w = refs[10:]
    place_tables(tab, idx, most)
    step = Step(ext, res)

    @pl.loop(0, 6)
    def fill(t):
        lanes = pl.ds(pl.multiple_of(t * LANES, LANES), LANES)
        step.place(t, lambda p: read_plane(raw, p, slice(None), lanes), "own")

    lane = iota((BLOCK, LANES), 1)
    to_east = to_west = jnp.zeros((BLOCK, LANES), F32)
    for p in range(PLANES):
        here = (lane >= 4 * p) & (lane < 4 * p + 4)
        east = read_plane(raw, p, slice(None), slice(640, 768))
        west = read_plane(raw, p, slice(None), slice(0, 128))
        edge[p, 0:48] = jnp.where(lane < 64, roll(east, 60, 1), roll(west, 68, 1))
        to_east = jnp.where(here, roll(east, 4 * p + 4, 1), to_east)
        to_west = jnp.where(here, roll(west, 4 * p, 1), to_west)
    col_e[...] = to_east
    col_w[...] = to_west

    @pl.loop(1, 5)
    def inner(t):
        step.tracer(t, 16, 32)
        step.motion(t, 16, 32)


def middle_kernel(row_a, row_b, ext_in, res_in, edge_in, ext, res, edge):
    step = Step(ext, res)
    even_row = step.gx % 2 == 0
    lane = iota((8, LANES), 1)
    for t in range(6):
        lanes = slice(LANES * t, LANES * t + LANES)

        def planes(p, t=t, lanes=lanes):
            rows = slice(8 * (p % 7), 8 * (p % 7) + 8)
            a, b = row_a[rows, lanes], row_b[rows, lanes]
            x = halo_tile(jnp.where(even_row, a, b), jnp.where(even_row, b, a), p)
            if t == 0:
                edge[p, 48:56] = roll(x, 68, 1)
            if t == 5:
                edge[p, 48:56] = jnp.where(lane < 64, roll(x, 60, 1), edge[p, 48:56])
            return x

        step.place(t, planes, "halo")

    @pl.loop(1, 5)
    def rims(t):
        step.tracer(t, 8, 8)
        step.tracer(t, 48, 8)
        step.motion(t, 8, 8)
        step.motion(t, 48, 16)

    for t in (0, 5):
        step.tracer(t, 8, 48)
        step.motion(t, 8, 56)
    step.passes(range(6))


def finish_kernel(col_a, col_b, idx, edge, ext_in, res_in, ext, res, send, table, sem):
    copy = pltpu.make_async_copy(idx, table, sem)
    copy.start()
    step = Step(ext, res)
    even = step.gy % 2 == 0
    a, b = col_a[...], col_b[...]
    from_east, from_west = jnp.where(even, a, b), jnp.where(even, b, a)
    lane = iota((HT, LANES), 1)

    def planes(p):
        near = jnp.where(lane < 64, roll(from_east, 60 - 4 * p, 1), roll(from_west, 64 - 4 * p, 1))
        return jnp.where((lane >= 60) & (lane < 68), near, edge[p])

    step.place(6, planes, "all")
    step.tracer(6, 8, 48)
    step.motion(6, 8, 56)
    step.passes((6,))
    lane = iota((BLOCK, LANES), 1)
    for r in range(0, 576, BLOCK):
        rows = slice(r, r + BLOCK)
        x = res[6, rows]
        res[0, rows] = jnp.where(lane < 4, roll(x, 60, 1), res[0, rows])
        res[5, rows] = jnp.where(lane >= 124, roll(x, 68, 1), res[5, rows])
    copy.wait()
    cut_pieces(1, table, res, send)


def cut_kernel(idx, res, send):
    cut_pieces(2, idx, res, send)


def route_kernel(rounds, idx, got, send):
    lane = iota((36, LANES), 1)

    @pl.loop(0, 2)
    def targets(part):
        for j in range(8):
            d = part * 8 + j
            moved = []
            for s in range(SLOTS):
                slot = d * SLOTS + s
                first, after, inner = idx[0, slot], idx[1, slot], idx[2, slot]
                if rounds > 1:
                    first, after = (
                        x + PIECE * (x // PIECE) + PIECE * idx[6, slot] for x in (first, after)
                    )
                near = got[pl.ds(first, 36), :]
                far = got[pl.ds(after, 36), :]
                x = jnp.where(lane >= inner, near, far)
                moved.append(pltpu.roll(x, (48 * s + 256 - inner) & 127, 1))
            for i, x in enumerate(pack_tiles(moved)):
                send[d, 36 * i : 36 * i + 36] = x


def settle_kernel(idx, got, heat, zonal, merid, height, east, north):
    used = jnp.broadcast_to(idx[5:6, :], (8, LANES))
    lane = iota((8, LANES), 1)
    low = iota((8, LANES), 0) < 4
    outs = (heat, zonal, merid, height, east, north)

    def put(tile_row, i, x):
        x = jnp.where(lane + LANES * i < used, x, 0.0)
        plane, rows = tile_row // 6, slice(8 * (tile_row % 6), 8 * (tile_row % 6) + 8)
        lanes = slice(LANES * i, LANES * i + LANES)
        if plane < 9:
            outs[plane // 3][plane % 3, rows, lanes] = x
        else:
            outs[plane - 6][rows, lanes] = x

    for i in range(3):
        for k in range(ROW_DEVICES):
            for t in range(4):
                put(4 * k + t, i, got[k, 36 * i + 8 * t : 36 * i + 8 * t + 8, :])
        for q in range(8):
            a = got[2 * q, 36 * i + 32 : 36 * i + 40, :]
            b = got[2 * q + 1, 36 * i + 28 : 36 * i + 36, :]
            put(64 + q, i, jnp.where(low, a, b))


def f32(*shape):
    return jax.ShapeDtypeStruct(shape, F32)


def cost(us):
    return pl.CostEstimate(flops=us * 1_000_000, bytes_accessed=us * 2_000_000, transcendentals=0)


VM = pl.BlockSpec(memory_space=pltpu.VMEM)
SM = pl.BlockSpec(memory_space=pltpu.SMEM)


def shards(heat, zonal, merid, height, east, north, depth, marine, sequence):
    raw = (heat, zonal, merid, height, east, north, depth, marine)
    tab = sequence.reshape(GRID_ROWS, LANES)

    def call(kernel, operands, ins, outs, shapes, mega=8, us=0, **more):
        more = {"in_specs": ins, "out_specs": outs, **more}
        return pl.pallas_call(
            kernel,
            out_shape=shapes,
            compiler_params=pltpu.CompilerParams(vmem_limit_bytes=mega << 20 if mega < 64 else 67_043_328),
            cost_estimate=cost(us) if us else None,
            **more,
        )(*operands)

    strips = [pltpu.VMEM(x.shape[:-2] + (8, 768), x.dtype) for _ in range(2) for x in raw]
    row_a, row_b = call(
        edge_kernel,
        tuple(pltpu.with_memory_space_constraint(x, pltpu.HBM) for x in raw),
        [pl.BlockSpec(memory_space=pltpu.HBM)] * 8,
        (VM, VM),
        (f32(56, 768), f32(56, 768)),
        mega=4,
        scratch_shapes=strips + [pltpu.SemaphoreType.DMA((16,))],
    )
    fields = (f32(FIELDS, STRIPS, STRIP, LANES), f32(STRIPS, 576, LANES))
    ints = jax.ShapeDtypeStruct((8, LANES), I32), jax.ShapeDtypeStruct((1, 1), I32)
    rim = f32(PLANES, HT, LANES)
    side = f32(BLOCK, LANES)
    ext, res, idx, most, edge, col_e, col_w = call(
        interior_kernel,
        (tab, row_a) + raw,
        [VM] * 10,
        (VM,) * 7,
        fields + ints + (rim, side, side),
        us=3,
    )

    def swaps(axis, size, first, second):
        near = [(i, i ^ 1) for i in range(size)]
        far = [(i, i + 1) for i in range(1, size - 1, 2)]
        far += [(j, i) for i, j in far]
        second = lax.ppermute(second, axis, far)
        first = lax.ppermute(first, axis, near)
        return first, second

    row_a, row_b = swaps("gx", GRID_ROWS, row_a, row_b)
    col_a, col_b = call(
        column_kernel,
        (row_a, row_b, col_e, col_w),
        [VM] * 4,
        (VM, VM),
        (f32(56, 128), f32(56, 128)),
        mega=4,
    )
    ext, res, edge = call(
        middle_kernel,
        (row_a, row_b, ext, res, edge),
        [VM] * 5,
        (VM,) * 3,
        fields + (rim,),
        us=3,
        input_output_aliases={2: 0, 3: 1, 4: 2},
    )
    col_a, col_b = swaps("gy", ROW_DEVICES, col_a, col_b)
    _, res, send = call(
        finish_kernel,
        (col_a, col_b, idx, edge, ext, res),
        [VM] * 6,
        (VM,) * 3,
        fields + (f32(ROW_DEVICES, PIECE, LANES),),
        us=2,
        input_output_aliases={4: 0, 5: 1},
        scratch_shapes=[pltpu.SMEM((8, LANES), I32), pltpu.SemaphoreType.DMA],
    )

    def deliver(rounds, send):
        got = lax.all_to_all(send, "gy", 0, 0, tiled=True)
        got = got.reshape(ROW_DEVICES * rounds * PIECE, LANES)
        piece = f32(ROW_DEVICES, PIECE, LANES)
        send = call(functools.partial(route_kernel, rounds), (idx, got), [SM, VM], VM, piece)
        got = lax.all_to_all(send, "gy", 0, 0, tiled=True)
        shapes = (f32(3, 48, 384),) * 3 + (f32(48, 384),) * 3
        return call(settle_kernel, (idx, got), [VM, VM], (VM,) * 6, shapes)

    def crowded():
        both = f32(ROW_DEVICES, 2 * PIECE, LANES)
        return deliver(2, call(cut_kernel, (idx, res), [SM, VM], VM, both))

    return lax.cond(most[0, 0] > 8, crowded, lambda: deliver(1, send))


def solution(mesh):
    level, flat = P(None, "gx", "gy"), P("gx", "gy")
    return jax.shard_map(
        shards,
        mesh=mesh,
        in_specs=(level,) * 3 + (flat,) * 5 + (P(),),
        out_specs=(P(None, None, ("gx", "gy")),) * 3 + (P(None, ("gx", "gy")),) * 3,
        check_vma=False,
    )
```

profile of v0, /device:TPU:0, one launch (start us, length us, event | category | flops | bytes accessed | tf_op | source)
XLA Modules:
  0.0 61.9 jit_solution(6445598139519889282)
XLA Ops:
  0.6 0.0 copy-start.7
  0.6 0.0 copy-start.6
  0.7 0.0 copy-start.5
  0.7 0.0 copy-start.4
  0.7 0.0 copy-start.3
  0.7 0.0 copy-start.2
  0.7 0.0 copy-start.1
  0.7 0.0 copy-start
  0.7 0.0 copy-start.8
  0.7 1.4 %shard_map.148 = (f32[56,768]{1,0:T(8,128)S(1)}, f32[56,768]{1,0:T(8,128)S(1)}) custom-call(f32[3,48,768]{2,1,0:T(8,128)} %refs_2_.3, f32[3,48,768]{2,1,0:T(8,128)} %refs_3_.3, f32[3,48,768]{2,1,0:T(8,128)} %refs_4_.3, f32[48,768]{1,0:T(8,128)} %refs_5_.3, f32[48,768]{1,0:T(8,128)} %refs_6_.3, f32[48,768]{1,0:T(8,128)} %refs_7_.3, f32[48,768]{1,0:T(8,128)} %refs_8_.1, ...), custom_call_target="tpu_custom_call" | custom-call | tf_op jit(solution)/shard_map/pallas_call | solution.py:502
  2.2 0.7 %collective-permute-start.1 = (f32[56,768]{1,0:T(8,128)S(1)}, f32[56,768]{1,0:T(8,128)S(1)}, u32[]{:S(2)}, u32[]{:S(2)}) collective-permute-start(f32[56,768]{1,0:T(8,128)S(1)} %get-tuple-element.36), channel_id=1, source_target_pairs={{16,32},{48,64},{80,96},{32,16},{64,48},{96,80},{17,33},{49,65},{8... | collective-permute-start | bytes 516104 | tf_op jit(solution)/shard_map/ppermute | solution.py:537
  2.8 3.0 %collective-permute-start = (f32[56,768]{1,0:T(8,128)S(1)}, f32[56,768]{1,0:T(8,128)S(1)}, u32[]{:S(2)}, u32[]{:S(2)}) collective-permute-start(f32[56,768]{1,0:T(8,128)S(1)} %get-tuple-element.34.refs_1_), channel_id=1, source_target_pairs={{0,16},{16,0},{32,48},{48,32},{64,80},{80,64},{96,112},{112,96},{1... | collective-permute-start | bytes 516104 | tf_op jit(solution)/shard_map/ppermute | solution.py:538
  5.9 0.0 copy-done.7
  5.9 0.0 copy-done.6
  5.9 0.0 copy-done.5
  5.9 0.0 copy-done.4
  5.9 0.0 copy-done.3
  5.9 2.0 %shard_map.149 = (f32[31,7,72,128]{3,2,1,0:T(8,128)S(1)}, f32[7,576,128]{2,1,0:T(8,128)S(1)}, s32[8,128]{1,0:T(8,128)S(1)}, s32[1,1]{1,0:T(1,128)}, f32[14,56,12...) custom-call(s32[8,128]{1,0:T(8,128)S(1)} %bitcast.6, f32[56,768]{1,0:T(8,128)S(1)} %get-tuple-element.34.refs_1_, ...), custom_call_target="tpu_custom_call" | custom-call | flops 3000000 | bytes 6000000 | tf_op jit(solution)/shard_map/pallas_call | solution.py:502
  8.0 0.0 collective-permute-done.1.row_b
  8.0 0.0 collective-permute-done.row_a
  8.0 0.1 shard_map.150
  8.1 1.7 %collective-permute-start.2 = (f32[56,128]{1,0:T(8,128)S(1)}, f32[56,128]{1,0:T(8,128)S(1)}, u32[]{:S(2)}, u32[]{:S(2)}) collective-permute-start(f32[56,128]{1,0:T(8,128)S(1)} %get-tuple-element.39), channel_id=1, source_target_pairs={{0,1},{1,0},{2,3},{3,2},{4,5},{5,4},{6,7},{7,6},{8,9},{9,8},{10,11... | collective-permute-start | bytes 86024 | tf_op jit(solution)/shard_map/ppermute | solution.py:538
  9.7 0.7 %collective-permute-start.3 = (f32[56,128]{1,0:T(8,128)S(1)}, f32[56,128]{1,0:T(8,128)S(1)}, u32[]{:S(2)}, u32[]{:S(2)}) collective-permute-start(f32[56,128]{1,0:T(8,128)S(1)} %get-tuple-element.40), channel_id=1, source_target_pairs={{1,2},{3,4},{5,6},{7,8},{9,10},{11,12},{13,14},{2,1},{4,3},{6,5},{... | collective-permute-start | bytes 86024 | tf_op jit(solution)/shard_map/ppermute | solution.py:537
  11.0 1.6 %shard_map.151 = (f32[31,7,72,128]{3,2,1,0:T(8,128)S(1)}, f32[7,576,128]{2,1,0:T(8,128)S(1)}, f32[14,56,128]{2,1,0:T(8,128)S(1)}) custom-call(f32[56,768]{1,0:T(8,128)S(1)} %collective-permute-done.row_a, f32[56,768]{1,0:T(8,128)S(1)} %collective-permute-done.1.row_b, ...), custom_call_target="tpu_custom_call", output_to_operand_aliasing={{0}: (2, {}), {1}: (3, {}), {2}: (4, {})} | custom-call | flops 3000000 | bytes 6000000 | tf_op jit(solution)/shard_map/pallas_call | solution.py:502
  12.6 0.0 collective-permute-done.2.col_a
  12.6 0.0 collective-permute-done.3.col_b
  12.6 2.0 %shard_map.152 = (f32[31,7,72,128]{3,2,1,0:T(8,128)S(1)}, f32[7,576,128]{2,1,0:T(8,128)S(1)}, f32[16,112,128]{2,1,0:T(8,128)S(1)}) custom-call(f32[56,128]{1,0:T(8,128)S(1)} %collective-permute-done.2.col_a, f32[56,128]{1,0:T(8,128)S(1)} %collective-permute-done.3.col_b, ...), custom_call_target="tpu_custom_call", output_to_operand_aliasing={{0}: (4, {}), {1}: (5, {})} | custom-call | flops 2000000 | bytes 4000000 | tf_op jit(solution)/shard_map/pallas_call | solution.py:502
  14.6 47.3 %conditional.1 = ((f32[3,48,384]{2,1,0:T(8,128)}, f32[3,48,384]{2,1,0:T(8,128)}, f32[3,48,384]{2,1,0:T(8,128)}, f32[48,384]{1,0:T(8,128)}, f32[48,384]{1,0:T(8,128)}, /*index=5*/f32[48,384]{1,0:T(8,128)})) conditional(s32[]{:T(128)} %bitcast.3, (f32[16,112,128]{2,1,0:T(8,128)S(1)}, s32[8,128]{1,0:T(8,128)S(1)}) %tuple.13, (s32[8,128]{1,0:T(8,128)S(1)}, ...), branch_computations={%region_0.0_spmd, %region_1.0_spmd} | conditional | bytes 5505032 | solution.py:584
  14.7 27.0 %all_to_all.16 = f32[16,112,128]{2,1,0:T(8,128)S(1)} all-to-all(f32[16,112,128]{2,1,0:T(8,128)S(1)} %get-tuple-element.9), channel_id=1, replica_groups=mesh['gx'=8,'gy'=16] {'gy'}, dimensions={0} | all-to-all | bytes 1835008 | tf_op jit(solution)/shard_map/cond/branch_0_fun/all_to_all | solution.py:572
  41.7 1.4 %branch_0_fun.2 = f32[16,112,128]{2,1,0:T(8,128)S(1)} custom-call(s32[8,128]{1,0:T(8,128)S(1)} %get-tuple-element.8.idx, f32[1792,128]{1,0:T(8,128)S(1)} %bitcast.5), custom_call_target="tpu_custom_call" | custom-call | tf_op jit(solution)/shard_map/cond/branch_0_fun/pallas_call | solution.py:502
  43.1 17.8 %all_to_all.17.got = f32[16,112,128]{2,1,0:T(8,128)S(1)} all-to-all(f32[16,112,128]{2,1,0:T(8,128)S(1)} %branch_0_fun.2), channel_id=1, replica_groups=mesh['gx'=8,'gy'=16] {'gy'}, dimensions={0} | all-to-all | bytes 1835008 | tf_op jit(solution)/shard_map/cond/branch_0_fun/all_to_all | solution.py:576
  60.9 1.0 %branch_0_fun.3 = (f32[3,48,384]{2,1,0:T(8,128)}, f32[3,48,384]{2,1,0:T(8,128)}, f32[3,48,384]{2,1,0:T(8,128)}, f32[48,384]{1,0:T(8,128)}, f32[48,384]{1,0:T(8,128)}, /*index=5*/f32[48,384]{1,0:T(8,128)}) custom-call(s32[8,128]{1,0:T(8,128)S(1)} %get-tuple-element.8.idx, f32[16,112,128]{2,1,0:T(8,128)S(1)} %all_to_all.17.got), custom_call_target="tpu_custom_call" | custom-call | tf_op jit(solution)/shard_map/cond/branch_0_fun/pallas_call | solution.py:502
  (4 shorter events, 0.0 us)
Async XLA Ops:
  0.6 5.2 %copy-start.7 = (s32[48,768]{1,0:T(8,128)S(1)}, s32[48,768]{1,0:T(8,128)}, u32[]{:S(2)}) copy-start(s32[48,768]{1,0:T(8,128)} %refs_9_.1) | copy-start | bytes 442372
  0.6 5.2 %copy-start.6 = (f32[48,768]{1,0:T(8,128)S(1)}, f32[48,768]{1,0:T(8,128)}, u32[]{:S(2)}) copy-start(f32[48,768]{1,0:T(8,128)} %refs_8_.1) | copy-start | bytes 442372
  0.7 5.2 %copy-start.5 = (f32[48,768]{1,0:T(8,128)S(1)}, f32[48,768]{1,0:T(8,128)}, u32[]{:S(2)}) copy-start(f32[48,768]{1,0:T(8,128)} %refs_7_.3) | copy-start | bytes 442372
  0.7 5.2 %copy-start.4 = (f32[48,768]{1,0:T(8,128)S(1)}, f32[48,768]{1,0:T(8,128)}, u32[]{:S(2)}) copy-start(f32[48,768]{1,0:T(8,128)} %refs_6_.3) | copy-start | bytes 442372
  0.7 5.2 %copy-start.3 = (f32[48,768]{1,0:T(8,128)S(1)}, f32[48,768]{1,0:T(8,128)}, u32[]{:S(2)}) copy-start(f32[48,768]{1,0:T(8,128)} %refs_5_.3) | copy-start | bytes 442372
  0.7 5.2 %copy-start.2 = (f32[3,48,768]{2,1,0:T(8,128)S(1)}, f32[3,48,768]{2,1,0:T(8,128)}, u32[]{:S(2)}) copy-start(f32[3,48,768]{2,1,0:T(8,128)} %refs_4_.3) | copy-start | bytes 1327108
  0.7 5.2 %copy-start.1 = (f32[3,48,768]{2,1,0:T(8,128)S(1)}, f32[3,48,768]{2,1,0:T(8,128)}, u32[]{:S(2)}) copy-start(f32[3,48,768]{2,1,0:T(8,128)} %refs_3_.3) | copy-start | bytes 1327108
  0.7 5.2 %copy-start = (f32[3,48,768]{2,1,0:T(8,128)S(1)}, f32[3,48,768]{2,1,0:T(8,128)}, u32[]{:S(2)}) copy-start(f32[3,48,768]{2,1,0:T(8,128)} %refs_2_.3) | copy-start | bytes 1327108
  0.7 5.2 %copy-start.8 = (s32[1024]{0:T(1024)S(1)}, s32[1024]{0:T(1024)}, u32[]{:S(2)}) copy-start(s32[1024]{0:T(1024)} %param.19) | copy-start | bytes 12292
  2.2 5.8 %collective-permute-start.1 = (f32[56,768]{1,0:T(8,128)S(1)}, f32[56,768]{1,0:T(8,128)S(1)}, u32[]{:S(2)}, u32[]{:S(2)}) collective-permute-start(f32[56,768]{1,0:T(8,128)S(1)} %get-tuple-element.36), channel_id=1, source_target_pairs={{16,32},{48,64},{80,96},{32,16},{64,48},{96,80},{17,33},{49,65},{8... | collective-permute-start | bytes 516104 | tf_op jit(solution)/shard_map/ppermute | solution.py:537
  2.8 5.1 %collective-permute-start = (f32[56,768]{1,0:T(8,128)S(1)}, f32[56,768]{1,0:T(8,128)S(1)}, u32[]{:S(2)}, u32[]{:S(2)}) collective-permute-start(f32[56,768]{1,0:T(8,128)S(1)} %get-tuple-element.34.refs_1_), channel_id=1, source_target_pairs={{0,16},{16,0},{32,48},{48,32},{64,80},{80,64},{96,112},{112,96},{1... | collective-permute-start | bytes 516104 | tf_op jit(solution)/shard_map/ppermute | solution.py:538
  8.1 4.5 %collective-permute-start.2 = (f32[56,128]{1,0:T(8,128)S(1)}, f32[56,128]{1,0:T(8,128)S(1)}, u32[]{:S(2)}, u32[]{:S(2)}) collective-permute-start(f32[56,128]{1,0:T(8,128)S(1)} %get-tuple-element.39), channel_id=1, source_target_pairs={{0,1},{1,0},{2,3},{3,2},{4,5},{5,4},{6,7},{7,6},{8,9},{9,8},{10,11... | collective-permute-start | bytes 86024 | tf_op jit(solution)/shard_map/ppermute | solution.py:538
  9.7 2.9 %collective-permute-start.3 = (f32[56,128]{1,0:T(8,128)S(1)}, f32[56,128]{1,0:T(8,128)S(1)}, u32[]{:S(2)}, u32[]{:S(2)}) collective-permute-start(f32[56,128]{1,0:T(8,128)S(1)} %get-tuple-element.40), channel_id=1, source_target_pairs={{1,2},{3,4},{5,6},{7,8},{9,10},{11,12},{13,14},{2,1},{4,3},{6,5},{... | collective-permute-start | bytes 86024 | tf_op jit(solution)/shard_map/ppermute | solution.py:537
where the time goes:
time: 62.1 us; the launch traced here: 61.9 us
  blocking collectives  44.8 us (72%)
  Pallas kernels  9.53 us (15%)
  starting transfers between devices  6.01 us (10%)
  between operations  1.46 us (2%)
    all_to_all x2, blocking collectives, deliver(): got = lax.all_to_all(send, 'gy', 0, 0, tiled=True)  44.8 us
    pallas_call x7, Pallas kernels, call(): pl.pallas_call(kernel, out_shape=shapes, compiler_params=pltpu.CompilerPa...  9.53 us
    ppermute x2, starting transfers between devices, swaps(): first = lax.ppermute(first, axis, near)  4.69 us
    ppermute x2, starting transfers between devices, swaps(): second = lax.ppermute(second, axis, far)  1.32 us
  transfers between devices with their start and end apart: 4, of which 0 were waited for; matrix products, arithmetic and copies ran while one was open for 0% of the time, Pallas kernels for 6%

commit v1 on v0

--- a/solution.py
+++ b/solution.py
@@ -163,15 +163,15 @@
 
 
 class Step:
-    def __init__(self, ext, res):
-        self.ext, self.res = ext, res
+    def __init__(self, ext, res, first=0):
+        self.ext, self.res, self.zero = ext, res, first
         self.gx, self.gy = lax.axis_index("gx"), lax.axis_index("gy")
 
     def put(self, field, t, x, first=8):
-        self.ext[field, t, first : first + x.shape[0]] = x
+        self.ext[field, t - self.zero, first : first + x.shape[0]] = x
 
     def mid(self, field, t, first=8, rows=HT):
-        return self.ext[field, t, first : first + rows]
+        return self.ext[field, t - self.zero, first : first + rows]
 
     def right(self, field, t, x, k=1, first=8):
         after = t if isinstance(t, int) and t in (5, 6) else t + 1
@@ -242,7 +242,7 @@
             ring = 0.1 * ((xe + xw) + (xn + xs))
             u, v = mid(U0 + q, first=first), mid(V0 + q, first=first)
             new = 0.6 * x + ring + (u * dx + v * dy)
-            self.res[t, 48 * q + first - 8 : 48 * q + first - 8 + rows] = wet * new
+            self.res[t - self.zero, 48 * q + first - 8 : 48 * q + first - 8 + rows] = wet * new
 
     def motion(self, t, first, rows):
         row = iota((rows, LANES), 0) + (first - 8)
@@ -264,8 +264,8 @@
             new_u = wet * ((0.6 * u + turn * v) + (side_x + ring_u))
             new_v = wet * ((0.6 * v - turn * u) + (side_y + ring_v))
             spot = 144 + 48 * q + first - 8
-            self.res[t, spot : spot + kept] = new_u[:kept]
-            self.res[t, spot + 144 : spot + 144 + kept] = new_v[:kept]
+            self.res[t - self.zero, spot : spot + kept] = new_u[:kept]
+            self.res[t - self.zero, spot + 144 : spot + 144 + kept] = new_v[:kept]
             du, dv = new_u - u, new_v - v
             gain_x = du if gain_x is None else gain_x + du
             gain_y = dv if gain_y is None else gain_y + dv
@@ -285,7 +285,7 @@
                 put(E0, t, new[48:56], 0)
                 put(E0, t, new[0:8], 64)
                 if last:
-                    self.res[t, 432:480] = new[:48]
+                    self.res[t - self.zero, 432:480] = new[:48]
             for t in strips:
                 e, quarter = mid(E0, t), mid(QUARTER, t)
                 ex = self.right(E0, t, e) - self.left(E0, t, e)
@@ -293,8 +293,8 @@
                 new_p = (mid(P0, t) + mid(GX, t)) - quarter * ex
                 new_q = (mid(Q0, t) + mid(GY, t)) - quarter * ey
                 if last:
-                    self.res[t, 480:528] = new_p[:48]
-                    self.res[t, 528:576] = new_q[:48]
+                    self.res[t - self.zero, 480:528] = new_p[:48]
+                    self.res[t - self.zero, 528:576] = new_q[:48]
                 else:
                     cross = mid(DEPTH, t) * new_q
                     put(P0, t, new_p)
@@ -370,7 +370,11 @@
         step.motion(t, 16, 32)
 
 
-def middle_kernel(row_a, row_b, ext_in, res_in, edge_in, ext, res, edge):
+def middle_kernel(
+    row_a, row_b, idx, ext_in, res_in, edge_in, ext, res, edge, send, table, sem
+):
+    copy = pltpu.make_async_copy(idx, table, sem)
+    copy.start()
     step = Step(ext, res)
     even_row = step.gx % 2 == 0
     lane = iota((8, LANES), 1)
@@ -400,12 +404,14 @@
         step.tracer(t, 8, 48)
         step.motion(t, 8, 56)
     step.passes(range(6))
-
-
-def finish_kernel(col_a, col_b, idx, edge, ext_in, res_in, ext, res, send, table, sem):
+    copy.wait()
+    cut_pieces(1, table, res, send)
+
+
+def finish_kernel(col_a, col_b, idx, edge, send_in, send, res, ext, table, sem):
     copy = pltpu.make_async_copy(idx, table, sem)
     copy.start()
-    step = Step(ext, res)
+    step = Step(ext, res, 6)
     even = step.gy % 2 == 0
     a, b = col_a[...], col_b[...]
     from_east, from_west = jnp.where(even, a, b), jnp.where(even, b, a)
@@ -419,24 +425,42 @@
     step.tracer(6, 8, 48)
     step.motion(6, 8, 56)
     step.passes((6,))
-    lane = iota((BLOCK, LANES), 1)
+    copy.wait()
+
+    last = jnp.int32(8)
+    for c in range(8):
+        last = jnp.where(table[3, c] == 15, c, last)
+    off = 48 * jnp.minimum(last, 7) + 44
+    rows = pl.ds(36 * (off >> 7), 36)
+    inner = off & 127
+    west = jnp.where(table[3, 0] == 0, 4, 0)
+    east = jnp.where(last < 8, 4, 0)
+    lane = iota((36, LANES), 1)
+    on_west, on_east = lane < west, (lane >= inner) & (lane < inner + east)
+    for k in range(ROW_DEVICES):
+        x = jnp.concatenate(
+            [res[0, 32 * k : 32 * k + 32], res[0, 512 + 4 * k : 516 + 4 * k]], axis=0
+        )
+        send[k, 0:36] = jnp.where(on_west, roll(x, 60, 1), send[k, 0:36])
+        moved = pltpu.roll(x, (inner + 72) & 127, 1)
+        send[k, rows, :] = jnp.where(on_east, moved, send[k, rows, :])
+
+
+def cut_kernel(idx, res, rim, send, whole):
+    for t in range(6):
+        whole[t] = res[t]
     for r in range(0, 576, BLOCK):
         rows = slice(r, r + BLOCK)
-        x = res[6, rows]
-        res[0, rows] = jnp.where(lane < 4, roll(x, 60, 1), res[0, rows])
-        res[5, rows] = jnp.where(lane >= 124, roll(x, 68, 1), res[5, rows])
-    copy.wait()
-    cut_pieces(1, table, res, send)
-
-
-def cut_kernel(idx, res, send):
-    cut_pieces(2, idx, res, send)
+        lane = iota((BLOCK, LANES), 1)
+        x = rim[0, rows]
+        whole[0, rows] = jnp.where(lane < 4, roll(x, 60, 1), res[0, rows])
+        whole[5, rows] = jnp.where(lane >= 124, roll(x, 68, 1), res[5, rows])
+    cut_pieces(2, idx, whole, send)
 
 
 def route_kernel(rounds, idx, got, send):
     lane = iota((36, LANES), 1)
 
-    @pl.loop(0, 2)
     def targets(part):
         for j in range(8):
             d = part * 8 + j
@@ -454,6 +478,12 @@
                 moved.append(pltpu.roll(x, (48 * s + 256 - inner) & 127, 1))
             for i, x in enumerate(pack_tiles(moved)):
                 send[d, 36 * i : 36 * i + 36] = x
+
+    if rounds == 1:
+        for part in range(2):
+            targets(part)
+    else:
+        pl.loop(0, 2)(targets)
 
 
 def settle_kernel(idx, got, heat, zonal, merid, height, east, north):
@@ -547,31 +577,33 @@
         (f32(56, 128), f32(56, 128)),
         mega=4,
     )
-    ext, res, edge = call(
+    piece = f32(ROW_DEVICES, PIECE, LANES)
+    table = [pltpu.SMEM((8, LANES), I32), pltpu.SemaphoreType.DMA]
+    ext, res, edge, send = call(
         middle_kernel,
-        (row_a, row_b, ext, res, edge),
-        [VM] * 5,
-        (VM,) * 3,
-        fields + (rim,),
+        (row_a, row_b, idx, ext, res, edge),
+        [VM] * 6,
+        (VM,) * 4,
+        fields + (rim, piece),
         us=3,
-        input_output_aliases={2: 0, 3: 1, 4: 2},
+        input_output_aliases={3: 0, 4: 1, 5: 2},
+        scratch_shapes=table,
     )
     col_a, col_b = swaps("gy", ROW_DEVICES, col_a, col_b)
-    _, res, send = call(
+    send, outer = call(
         finish_kernel,
-        (col_a, col_b, idx, edge, ext, res),
-        [VM] * 6,
-        (VM,) * 3,
-        fields + (f32(ROW_DEVICES, PIECE, LANES),),
+        (col_a, col_b, idx, edge, send),
+        [VM] * 5,
+        (VM,) * 2,
+        (piece, f32(1, 576, LANES)),
         us=2,
-        input_output_aliases={4: 0, 5: 1},
-        scratch_shapes=[pltpu.SMEM((8, LANES), I32), pltpu.SemaphoreType.DMA],
+        input_output_aliases={4: 0},
+        scratch_shapes=[pltpu.VMEM((FIELDS, 1, STRIP, LANES), F32)] + table,
     )
 
     def deliver(rounds, send):
         got = lax.all_to_all(send, "gy", 0, 0, tiled=True)
         got = got.reshape(ROW_DEVICES * rounds * PIECE, LANES)
-        piece = f32(ROW_DEVICES, PIECE, LANES)
         send = call(functools.partial(route_kernel, rounds), (idx, got), [SM, VM], VM, piece)
         got = lax.all_to_all(send, "gy", 0, 0, tiled=True)
         shapes = (f32(3, 48, 384),) * 3 + (f32(48, 384),) * 3
@@ -579,7 +611,9 @@
 
     def crowded():
         both = f32(ROW_DEVICES, 2 * PIECE, LANES)
-        return deliver(2, call(cut_kernel, (idx, res), [SM, VM], VM, both))
+        whole = [pltpu.VMEM((STRIPS, 576, LANES), F32)]
+        ins = [SM, VM, VM]
+        return deliver(2, call(cut_kernel, (idx, res, outer), ins, VM, both, scratch_shapes=whole))
 
     return lax.cond(most[0, 0] > 8, crowded, lambda: deliver(1, send))
 

time: 62.1 us -> 62 us (level)
  the two profiles are of different devices: /device:TPU:0 before, /device:TPU:1 now
where the time goes in v1:
time: 62 us; the launch traced here: 61.7 us
  blocking collectives  42.7 us (69%)
  Pallas kernels  9.24 us (15%)
  starting transfers between devices  6.73 us (11%)
  between operations  1.49 us (2%)
  waiting for transfers between devices  1.47 us (2%)
    all_to_all x2, blocking collectives, deliver(): got = lax.all_to_all(send, 'gy', 0, 0, tiled=True)  42.7 us
    pallas_call x7, Pallas kernels, call(): pl.pallas_call(kernel, out_shape=shapes, compiler_params=pltpu.CompilerPa...  9.24 us
    ppermute x2, starting transfers between devices, swaps(): second = lax.ppermute(second, axis, far)  3.78 us
    ppermute x2, starting transfers between devices, swaps(): first = lax.ppermute(first, axis, near)  2.95 us
    ppermute x2, waiting for transfers between devices, swaps(): second = lax.ppermute(second, axis, far)  1.47 us
  transfers between devices with their start and end apart: 4, of which 1 were waited for; matrix products, arithmetic and copies ran while one was open for 0% of the time, Pallas kernels for 7%

profile of v1, /device:TPU:1, one launch (start us, length us, event | category | flops | bytes accessed | tf_op | source)
XLA Modules:
  0.0 61.7 jit_solution(1258145472514379351)
XLA Ops:
  0.6 0.0 copy-start
  0.6 0.0 copy-start.1
  0.7 0.0 copy-start.2
  0.7 0.0 copy-start.3
  0.7 0.0 copy-start.4
  0.7 0.0 copy-start.5
  0.7 0.0 copy-start.6
  0.7 0.0 copy-start.7
  0.7 0.0 copy-start.8
  0.7 1.4 %shard_map.148 = (f32[56,768]{1,0:T(8,128)S(1)}, f32[56,768]{1,0:T(8,128)S(1)}) custom-call(f32[3,48,768]{2,1,0:T(8,128)} %refs_2_.3, f32[3,48,768]{2,1,0:T(8,128)} %refs_3_.3, f32[3,48,768]{2,1,0:T(8,128)} %refs_4_.3, f32[48,768]{1,0:T(8,128)} %refs_5_.3, f32[48,768]{1,0:T(8,128)} %refs_6_.3, f32[48,768]{1,0:T(8,128)} %refs_7_.3, f32[48,768]{1,0:T(8,128)} %refs_8_.1, ...), custom_call_target="tpu_custom_call" | custom-call | tf_op jit(solution)/shard_map/pallas_call | solution.py:532
  2.2 1.5 %collective-permute-start = (f32[56,768]{1,0:T(8,128)S(1)}, f32[56,768]{1,0:T(8,128)S(1)}, u32[]{:S(2)}, u32[]{:S(2)}) collective-permute-start(f32[56,768]{1,0:T(8,128)S(1)} %get-tuple-element.37.refs_1_), channel_id=1, source_target_pairs={{0,16},{16,0},{32,48},{48,32},{64,80},{80,64},{96,112},{112,96},{1... | collective-permute-start | bytes 516104 | tf_op jit(solution)/shard_map/ppermute | solution.py:568
  3.6 3.1 %collective-permute-start.1 = (f32[56,768]{1,0:T(8,128)S(1)}, f32[56,768]{1,0:T(8,128)S(1)}, u32[]{:S(2)}, u32[]{:S(2)}) collective-permute-start(f32[56,768]{1,0:T(8,128)S(1)} %get-tuple-element.39), channel_id=1, source_target_pairs={{16,32},{48,64},{80,96},{32,16},{64,48},{96,80},{17,33},{49,65},{8... | collective-permute-start | bytes 516104 | tf_op jit(solution)/shard_map/ppermute | solution.py:567
  6.8 0.0 copy-done
  6.8 0.0 copy-done.1
  6.8 0.0 copy-done.2
  6.8 0.0 copy-done.3
  6.8 0.0 copy-done.4
  6.8 2.0 %shard_map.149 = (f32[31,7,72,128]{3,2,1,0:T(8,128)S(1)}, f32[7,576,128]{2,1,0:T(8,128)S(1)}, s32[8,128]{1,0:T(8,128)S(1)}, s32[1,1]{1,0:T(1,128)}, f32[14,56,12...) custom-call(s32[8,128]{1,0:T(8,128)S(1)} %bitcast.6, f32[56,768]{1,0:T(8,128)S(1)} %get-tuple-element.37.refs_1_, ...), custom_call_target="tpu_custom_call" | custom-call | flops 3000000 | bytes 6000000 | tf_op jit(solution)/shard_map/pallas_call | solution.py:532
  8.9 0.0 collective-permute-done.row_a
  8.9 1.5 %collective-permute-done.1.row_b = f32[56,768]{1,0:T(8,128)S(1)} collective-permute-done((f32[56,768]{1,0:T(8,128)S(1)}, f32[56,768]{1,0:T(8,128)S(1)}, u32[]{:S(2)}, u32[]{:S(2)}) %collective-permute-start.1) | collective-permute-done | bytes 172064 | tf_op jit(solution)/shard_map/ppermute | solution.py:567
  10.3 0.1 shard_map.150
  10.4 1.5 %collective-permute-start.2 = (f32[56,128]{1,0:T(8,128)S(1)}, f32[56,128]{1,0:T(8,128)S(1)}, u32[]{:S(2)}, u32[]{:S(2)}) collective-permute-start(f32[56,128]{1,0:T(8,128)S(1)} %get-tuple-element.42), channel_id=1, source_target_pairs={{0,1},{1,0},{2,3},{3,2},{4,5},{5,4},{6,7},{7,6},{8,9},{9,8},{10,11... | collective-permute-start | bytes 86024 | tf_op jit(solution)/shard_map/ppermute | solution.py:568
  11.9 0.7 %collective-permute-start.3 = (f32[56,128]{1,0:T(8,128)S(1)}, f32[56,128]{1,0:T(8,128)S(1)}, u32[]{:S(2)}, u32[]{:S(2)}) collective-permute-start(f32[56,128]{1,0:T(8,128)S(1)} %get-tuple-element.43), channel_id=1, source_target_pairs={{1,2},{3,4},{5,6},{7,8},{9,10},{11,12},{13,14},{2,1},{4,3},{6,5},{... | collective-permute-start | bytes 86024 | tf_op jit(solution)/shard_map/ppermute | solution.py:567
  13.2 2.3 %shard_map.151 = (f32[31,7,72,128]{3,2,1,0:T(8,128)S(1)}, f32[7,576,128]{2,1,0:T(8,128)S(1)}, f32[14,56,128]{2,1,0:T(8,128)S(1)}, f32[16,112,128]{2,1,0:T(8,128)S(1)}) custom-call(f32[56,768]{1,0:T(8,128)S(1)} %collective-permute-done.row_a, f32[56,768]{1,0:T(8,128)S(1)} %collective-permute-done.1.row_b, ...), custom_call_target="tpu_custom_call", output_to_operand_aliasing={{0}: (3, {}), {1}: (4, {}), {2}: (5, {})} | custom-call | flops 3000000 | bytes 6000000 | tf_op jit(solution)/shard_map/pallas_call | solution.py:532
  15.5 0.0 collective-permute-done.2.col_a
  15.5 0.0 collective-permute-done.3.col_b
  15.5 1.1 %shard_map.152 = (f32[16,112,128]{2,1,0:T(8,128)S(1)}, f32[1,576,128]{2,1,0:T(8,128)S(1)}) custom-call(f32[56,128]{1,0:T(8,128)S(1)} %collective-permute-done.2.col_a, f32[56,128]{1,0:T(8,128)S(1)} %collective-permute-done.3.col_b, s32[8,128]{1,0:T(8,128)S(1)} %get-tuple-element.44.idx, ...), custom_call_target="tpu_custom_call", output_to_operand_aliasing={{0}: (4, {})} | custom-call | flops 2000000 | bytes 4000000 | tf_op jit(solution)/shard_map/pallas_call | solution.py:532
  16.6 45.1 %conditional.1 = ((f32[3,48,384]{2,1,0:T(8,128)}, f32[3,48,384]{2,1,0:T(8,128)}, f32[3,48,384]{2,1,0:T(8,128)}, f32[48,384]{1,0:T(8,128)}, f32[48,384]{1,0:T(8,128)}, /*index=5*/f32[48,384]{1,0:T(8,128)})) conditional(s32[]{:T(128)} %bitcast.3, (f32[16,112,128]{2,1,0:T(8,128)S(1)}, s32[8,128]{1,0:T(8,128)S(1)}) %tuple.13, (s32[8,128]{1,0:T(8,128)S(1)}, ...), branch_computations={%region_0.0_spmd, %region_1.0_spmd} | conditional | bytes 5505032 | solution.py:618
  16.6 23.8 %all_to_all.16 = f32[16,112,128]{2,1,0:T(8,128)S(1)} all-to-all(f32[16,112,128]{2,1,0:T(8,128)S(1)} %get-tuple-element.11), channel_id=1, replica_groups=mesh['gx'=8,'gy'=16] {'gy'}, dimensions={0} | all-to-all | bytes 1835008 | tf_op jit(solution)/shard_map/cond/branch_0_fun/all_to_all | solution.py:605
  40.4 1.4 %branch_0_fun.2 = f32[16,112,128]{2,1,0:T(8,128)S(1)} custom-call(s32[8,128]{1,0:T(8,128)S(1)} %get-tuple-element.10.idx, f32[1792,128]{1,0:T(8,128)S(1)} %bitcast.5), custom_call_target="tpu_custom_call" | custom-call | tf_op jit(solution)/shard_map/cond/branch_0_fun/pallas_call | solution.py:532
  41.8 19.0 %all_to_all.17.got = f32[16,112,128]{2,1,0:T(8,128)S(1)} all-to-all(f32[16,112,128]{2,1,0:T(8,128)S(1)} %branch_0_fun.2), channel_id=1, replica_groups=mesh['gx'=8,'gy'=16] {'gy'}, dimensions={0} | all-to-all | bytes 1835008 | tf_op jit(solution)/shard_map/cond/branch_0_fun/all_to_all | solution.py:608
  60.8 1.0 %branch_0_fun.3 = (f32[3,48,384]{2,1,0:T(8,128)}, f32[3,48,384]{2,1,0:T(8,128)}, f32[3,48,384]{2,1,0:T(8,128)}, f32[48,384]{1,0:T(8,128)}, f32[48,384]{1,0:T(8,128)}, /*index=5*/f32[48,384]{1,0:T(8,128)}) custom-call(s32[8,128]{1,0:T(8,128)S(1)} %get-tuple-element.10.idx, f32[16,112,128]{2,1,0:T(8,128)S(1)} %all_to_all.17.got), custom_call_target="tpu_custom_call" | custom-call | tf_op jit(solution)/shard_map/cond/branch_0_fun/pallas_call | solution.py:532
  (4 shorter events, 0.0 us)
Async XLA Ops:
  0.6 6.1 %copy-start = (f32[3,48,768]{2,1,0:T(8,128)S(1)}, f32[3,48,768]{2,1,0:T(8,128)}, u32[]{:S(2)}) copy-start(f32[3,48,768]{2,1,0:T(8,128)} %refs_2_.3) | copy-start | bytes 1327108
  0.6 6.1 %copy-start.1 = (f32[3,48,768]{2,1,0:T(8,128)S(1)}, f32[3,48,768]{2,1,0:T(8,128)}, u32[]{:S(2)}) copy-start(f32[3,48,768]{2,1,0:T(8,128)} %refs_3_.3) | copy-start | bytes 1327108
  0.7 6.1 %copy-start.2 = (f32[3,48,768]{2,1,0:T(8,128)S(1)}, f32[3,48,768]{2,1,0:T(8,128)}, u32[]{:S(2)}) copy-start(f32[3,48,768]{2,1,0:T(8,128)} %refs_4_.3) | copy-start | bytes 1327108
  0.7 6.1 %copy-start.3 = (f32[48,768]{1,0:T(8,128)S(1)}, f32[48,768]{1,0:T(8,128)}, u32[]{:S(2)}) copy-start(f32[48,768]{1,0:T(8,128)} %refs_5_.3) | copy-start | bytes 442372
  0.7 6.1 %copy-start.4 = (f32[48,768]{1,0:T(8,128)S(1)}, f32[48,768]{1,0:T(8,128)}, u32[]{:S(2)}) copy-start(f32[48,768]{1,0:T(8,128)} %refs_6_.3) | copy-start | bytes 442372
  0.7 6.1 %copy-start.5 = (f32[48,768]{1,0:T(8,128)S(1)}, f32[48,768]{1,0:T(8,128)}, u32[]{:S(2)}) copy-start(f32[48,768]{1,0:T(8,128)} %refs_7_.3) | copy-start | bytes 442372
  0.7 6.1 %copy-start.6 = (f32[48,768]{1,0:T(8,128)S(1)}, f32[48,768]{1,0:T(8,128)}, u32[]{:S(2)}) copy-start(f32[48,768]{1,0:T(8,128)} %refs_8_.1) | copy-start | bytes 442372
  0.7 6.1 %copy-start.7 = (s32[48,768]{1,0:T(8,128)S(1)}, s32[48,768]{1,0:T(8,128)}, u32[]{:S(2)}) copy-start(s32[48,768]{1,0:T(8,128)} %refs_9_.1) | copy-start | bytes 442372
  0.7 6.1 %copy-start.8 = (s32[1024]{0:T(1024)S(1)}, s32[1024]{0:T(1024)}, u32[]{:S(2)}) copy-start(s32[1024]{0:T(1024)} %param.19) | copy-start | bytes 12292
  2.2 6.7 %collective-permute-start = (f32[56,768]{1,0:T(8,128)S(1)}, f32[56,768]{1,0:T(8,128)S(1)}, u32[]{:S(2)}, u32[]{:S(2)}) collective-permute-start(f32[56,768]{1,0:T(8,128)S(1)} %get-tuple-element.37.refs_1_), channel_id=1, source_target_pairs={{0,16},{16,0},{32,48},{48,32},{64,80},{80,64},{96,112},{112,96},{1... | collective-permute-start | bytes 516104 | tf_op jit(solution)/shard_map/ppermute | solution.py:568
  3.6 6.7 %collective-permute-start.1 = (f32[56,768]{1,0:T(8,128)S(1)}, f32[56,768]{1,0:T(8,128)S(1)}, u32[]{:S(2)}, u32[]{:S(2)}) collective-permute-start(f32[56,768]{1,0:T(8,128)S(1)} %get-tuple-element.39), channel_id=1, source_target_pairs={{16,32},{48,64},{80,96},{32,16},{64,48},{96,80},{17,33},{49,65},{8... | collective-permute-start | bytes 516104 | tf_op jit(solution)/shard_map/ppermute | solution.py:567
  10.4 5.1 %collective-permute-start.2 = (f32[56,128]{1,0:T(8,128)S(1)}, f32[56,128]{1,0:T(8,128)S(1)}, u32[]{:S(2)}, u32[]{:S(2)}) collective-permute-start(f32[56,128]{1,0:T(8,128)S(1)} %get-tuple-element.42), channel_id=1, source_target_pairs={{0,1},{1,0},{2,3},{3,2},{4,5},{5,4},{6,7},{7,6},{8,9},{9,8},{10,11... | collective-permute-start | bytes 86024 | tf_op jit(solution)/shard_map/ppermute | solution.py:568
  11.9 3.6 %collective-permute-start.3 = (f32[56,128]{1,0:T(8,128)S(1)}, f32[56,128]{1,0:T(8,128)S(1)}, u32[]{:S(2)}, u32[]{:S(2)}) collective-permute-start(f32[56,128]{1,0:T(8,128)S(1)} %get-tuple-element.43), channel_id=1, source_target_pairs={{1,2},{3,4},{5,6},{7,8},{9,10},{11,12},{13,14},{2,1},{4,3},{6,5},{... | collective-permute-start | bytes 86024 | tf_op jit(solution)/shard_map/ppermute | solution.py:567

commit v2 on v1

--- a/solution.py
+++ b/solution.py
@@ -48,20 +48,28 @@
     return jnp.where(low, roll(north, 4, 0), south)
 
 
+EDGES = (
+    (slice(0, 8), slice(None)),
+    (slice(40, 48), slice(None)),
+    (slice(None), slice(0, 128)),
+    (slice(None), slice(640, 768)),
+)
+
+
 def edge_kernel(*refs):
     raw = refs[:8]
-    row_a, row_b = refs[8:10]
-    parts, sem = refs[10:26], refs[26]
+    row_a, row_b, col_a, col_b = refs[8:12]
+    parts, sem = refs[12:44], refs[44]
     copies = []
-    for i, rows in enumerate((slice(0, 8), slice(40, 48))):
+    for i in (2, 3, 0, 1):
         for j, x in enumerate(raw):
-            where = (slice(None),) * (len(x.shape) - 2) + (rows, slice(None))
+            where = (slice(None),) * (len(x.shape) - 2) + EDGES[i]
             n = 8 * i + j
             copies.append(pltpu.make_async_copy(x.at[where], parts[n], sem.at[n]))
-            copies[-1].start()
+            copies[-1].start(priority=1)
     for copy in copies:
         copy.wait()
-    bottoms, tops = parts[:8], parts[8:]
+    bottoms, tops, lefts, rights = (parts[8 * i : 8 * i + 8] for i in range(4))
     even = lax.axis_index("gx") % 2 == 0
     low = iota((8, 768), 0) < 4
     full = slice(None)
@@ -72,6 +80,15 @@
         bottom = jnp.where(low, b0, roll(b1, 4, 0))
         row_a[8 * m : 8 * m + 8] = jnp.where(even, top, bottom)
         row_b[8 * m : 8 * m + 8] = jnp.where(even, bottom, top)
+    even = lax.axis_index("gy") % 2 == 0
+    lane = iota((BLOCK, LANES), 1)
+    to_east = to_west = jnp.zeros((BLOCK, LANES), F32)
+    for p in range(PLANES):
+        here = (lane >= 4 * p) & (lane < 4 * p + 4)
+        to_east = jnp.where(here, roll(read_plane(rights, p, full, full), 4 * p + 4, 1), to_east)
+        to_west = jnp.where(here, roll(read_plane(lefts, p, full, full), 4 * p, 1), to_west)
+    col_a[...] = jnp.where(even, to_east, to_west)
+    col_b[...] = jnp.where(even, to_west, to_east)
 
 
 def place_tables(tab_ref, idx, full):
@@ -119,28 +136,19 @@
     full[...] = most[:, :1].astype(I32)
 
 
-def column_kernel(row_a, row_b, col_e, col_w, col_a, col_b):
-    gx, gy = lax.axis_index("gx"), lax.axis_index("gy")
-    even_row, even = gx % 2 == 0, gy % 2 == 0
+def corner_kernel(col_a, col_b, after, cor_a, cor_b):
+    even_row = lax.axis_index("gx") % 2 == 0
+    even = lax.axis_index("gy") % 2 == 0
     lane = iota((8, LANES), 1)
-    east = jnp.zeros((8, LANES), F32)
-    west = jnp.zeros((8, LANES), F32)
-    for p in range(PLANES):
-        rows = slice(8 * (p % 7), 8 * (p % 7) + 8)
-        here = (lane >= 4 * p) & (lane < 4 * p + 4)
-        w, e = (
-            halo_tile(jnp.where(even_row, a, b), jnp.where(even_row, b, a), p)
-            for a, b in (
-                (row_a[rows, i : i + LANES], row_b[rows, i : i + LANES]) for i in (0, 640)
-            )
-        )
-        east = jnp.where(here, roll(e, 4 * p + 4, 1), east)
-        west = jnp.where(here, roll(w, 4 * p, 1), west)
-    e_own, w_own = col_e[...], col_w[...]
-    col_a[0:48] = jnp.where(even, e_own, w_own)
-    col_b[0:48] = jnp.where(even, w_own, e_own)
-    col_a[48:56] = jnp.where(even, east, west)
-    col_b[48:56] = jnp.where(even, west, east)
+
+    def rows(first):
+        a, b = col_a[first : first + 8], col_b[first : first + 8]
+        east, west = jnp.where(even, a, b), jnp.where(even, b, a)
+        return jnp.where(lane < 64, east, roll(west, 64, 1))
+
+    top, bottom = roll(rows(40), 4, 0), rows(0)
+    cor_a[...] = jnp.where(even_row, top, bottom)
+    cor_b[...] = jnp.where(even_row, bottom, top)
 
 
 HT = 56
@@ -343,7 +351,7 @@
 
 def interior_kernel(*refs):
     tab, raw = refs[0], refs[2:10]
-    ext, res, idx, most, edge, col_e, col_w = refs[10:]
+    ext, res, idx, most, edge = refs[10:]
     place_tables(tab, idx, most)
     step = Step(ext, res)
 
@@ -353,16 +361,10 @@
         step.place(t, lambda p: read_plane(raw, p, slice(None), lanes), "own")
 
     lane = iota((BLOCK, LANES), 1)
-    to_east = to_west = jnp.zeros((BLOCK, LANES), F32)
     for p in range(PLANES):
-        here = (lane >= 4 * p) & (lane < 4 * p + 4)
         east = read_plane(raw, p, slice(None), slice(640, 768))
         west = read_plane(raw, p, slice(None), slice(0, 128))
         edge[p, 0:48] = jnp.where(lane < 64, roll(east, 60, 1), roll(west, 68, 1))
-        to_east = jnp.where(here, roll(east, 4 * p + 4, 1), to_east)
-        to_west = jnp.where(here, roll(west, 4 * p, 1), to_west)
-    col_e[...] = to_east
-    col_w[...] = to_west
 
     @pl.loop(1, 5)
     def inner(t):
@@ -408,13 +410,18 @@
     cut_pieces(1, table, res, send)
 
 
-def finish_kernel(col_a, col_b, idx, edge, send_in, send, res, ext, table, sem):
+def finish_kernel(col_a, col_b, cor_a, cor_b, idx, edge, send_in, send, res, ext, table, sem):
     copy = pltpu.make_async_copy(idx, table, sem)
     copy.start()
     step = Step(ext, res, 6)
     even = step.gy % 2 == 0
+    even_row = step.gx % 2 == 0
+    a, b = cor_a[...], cor_b[...]
+    north, south = jnp.where(even_row, a, b), jnp.where(even_row, b, a)
+    corner = jnp.where(iota((8, LANES), 0) < 4, north, roll(south, 4, 0))
     a, b = col_a[...], col_b[...]
-    from_east, from_west = jnp.where(even, a, b), jnp.where(even, b, a)
+    from_east = jnp.concatenate([jnp.where(even, a, b), corner], axis=0)
+    from_west = jnp.concatenate([jnp.where(even, b, a), roll(corner, 64, 1)], axis=0)
     lane = iota((HT, LANES), 1)
 
     def planes(p):
@@ -538,27 +545,24 @@
         )(*operands)
 
     strips = [pltpu.VMEM(x.shape[:-2] + (8, 768), x.dtype) for _ in range(2) for x in raw]
-    row_a, row_b = call(
+    strips += [pltpu.VMEM(x.shape[:-2] + (BLOCK, LANES), x.dtype) for _ in range(2) for x in raw]
+    row_a, row_b, col_a, col_b = call(
         edge_kernel,
         tuple(pltpu.with_memory_space_constraint(x, pltpu.HBM) for x in raw),
         [pl.BlockSpec(memory_space=pltpu.HBM)] * 8,
-        (VM, VM),
-        (f32(56, 768), f32(56, 768)),
+        (VM,) * 4,
+        (f32(56, 768), f32(56, 768), f32(BLOCK, LANES), f32(BLOCK, LANES)),
         mega=4,
-        scratch_shapes=strips + [pltpu.SemaphoreType.DMA((16,))],
+        scratch_shapes=strips + [pltpu.SemaphoreType.DMA((32,))],
     )
     fields = (f32(FIELDS, STRIPS, STRIP, LANES), f32(STRIPS, 576, LANES))
     ints = jax.ShapeDtypeStruct((8, LANES), I32), jax.ShapeDtypeStruct((1, 1), I32)
     rim = f32(PLANES, HT, LANES)
-    side = f32(BLOCK, LANES)
-    ext, res, idx, most, edge, col_e, col_w = call(
-        interior_kernel,
-        (tab, row_a) + raw,
-        [VM] * 10,
-        (VM,) * 7,
-        fields + ints + (rim, side, side),
-        us=3,
+    ext, res, idx, most, edge = call(
+        interior_kernel, (tab, row_a) + raw, [VM] * 10, (VM,) * 5, fields + ints + (rim,), us=3
     )
+
+    full = (most > 8).astype(I32)
 
     def swaps(axis, size, first, second):
         near = [(i, i ^ 1) for i in range(size)]
@@ -568,13 +572,14 @@
         first = lax.ppermute(first, axis, near)
         return first, second
 
+    col_a, col_b = swaps("gy", ROW_DEVICES, col_a, col_b)
     row_a, row_b = swaps("gx", GRID_ROWS, row_a, row_b)
-    col_a, col_b = call(
-        column_kernel,
-        (row_a, row_b, col_e, col_w),
-        [VM] * 4,
+    cor_a, cor_b = call(
+        corner_kernel,
+        (col_a, col_b, full),
+        [VM] * 3,
         (VM, VM),
-        (f32(56, 128), f32(56, 128)),
+        (f32(8, LANES), f32(8, LANES)),
         mega=4,
     )
     piece = f32(ROW_DEVICES, PIECE, LANES)
@@ -589,15 +594,15 @@
         input_output_aliases={3: 0, 4: 1, 5: 2},
         scratch_shapes=table,
     )
-    col_a, col_b = swaps("gy", ROW_DEVICES, col_a, col_b)
+    cor_a, cor_b = swaps("gx", GRID_ROWS, cor_a, cor_b)
     send, outer = call(
         finish_kernel,
-        (col_a, col_b, idx, edge, send),
-        [VM] * 5,
+        (col_a, col_b, cor_a, cor_b, idx, edge, send),
+        [VM] * 7,
         (VM,) * 2,
         (piece, f32(1, 576, LANES)),
         us=2,
-        input_output_aliases={4: 0},
+        input_output_aliases={6: 0},
         scratch_shapes=[pltpu.VMEM((FIELDS, 1, STRIP, LANES), F32)] + table,
     )
 
@@ -615,7 +620,7 @@
         ins = [SM, VM, VM]
         return deliver(2, call(cut_kernel, (idx, res, outer), ins, VM, both, scratch_shapes=whole))
 
-    return lax.cond(most[0, 0] > 8, crowded, lambda: deliver(1, send))
+    return lax.cond(full[0, 0] > 0, crowded, lambda: deliver(1, send))
 
 
 def solution(mesh):

time: 62 us -> 65.7 us (1.060)
  the two profiles are of different devices: /device:TPU:1 before, /device:TPU:4 now
where the time goes in v2:
time: 65.7 us; the launch traced here: 65.4 us
  blocking collectives  46.4 us (71%)
  Pallas kernels  9.47 us (14%)
  starting transfers between devices  7.71 us (12%)
  between operations  1.53 us (2%)
    all_to_all x2, blocking collectives, deliver(): got = lax.all_to_all(send, 'gy', 0, 0, tiled=True)  46.4 us
    pallas_call x7, Pallas kernels, call(): pl.pallas_call(kernel, out_shape=shapes, compiler_params=pltpu.CompilerPa...  9.47 us
    ppermute x3, starting transfers between devices, swaps(): second = lax.ppermute(second, axis, far)  5.54 us
    ppermute x3, starting transfers between devices, swaps(): first = lax.ppermute(first, axis, near)  2.17 us
  transfers between devices with their start and end apart: 6, of which 1 were waited for; matrix products, arithmetic and copies ran while one was open for 0% of the time, Pallas kernels for 6%

profile of v2, /device:TPU:4, one launch (start us, length us, event | category | flops | bytes accessed | tf_op | source)
XLA Modules:
  0.0 65.4 jit_solution(1635659001118476940)
XLA Ops:
  0.6 0.0 copy-start
  0.6 0.0 copy-start.1
  0.7 0.0 copy-start.2
  0.7 0.0 copy-start.3
  0.7 0.0 copy-start.4
  0.7 0.0 copy-start.5
  0.7 0.0 copy-start.6
  0.7 0.0 copy-start.7
  0.7 0.0 copy-start.8
  0.7 2.0 %shard_map.148 = (f32[56,768]{1,0:T(8,128)S(1)}, f32[56,768]{1,0:T(8,128)S(1)}, f32[48,128]{1,0:T(8,128)S(1)}, f32[48,128]{1,0:T(8,128)S(1)}) custom-call(f32[3,48,768]{2,1,0:T(8,128)} %refs_2_.3, f32[3,48,768]{2,1,0:T(8,128)} %refs_3_.3, f32[3,48,768]{2,1,0:T(8,128)} %refs_4_.3, f32[48,768]{1,0:T(8,128)} %refs_5_.3, f32[48,768]{1,0:T(8,128)} %refs_6_.3, ...), custom_call_target="tpu_custom_call" | custom-call | tf_op jit(solution)/shard_map/pallas_call | solution.py:539
  2.7 0.1 collective-permute-start.4
  2.8 2.5 %collective-permute-start.5 = (f32[56,768]{1,0:T(8,128)S(1)}, f32[56,768]{1,0:T(8,128)S(1)}, u32[]{:S(2)}, u32[]{:S(2)}) collective-permute-start(f32[56,768]{1,0:T(8,128)S(1)} %get-tuple-element.44), channel_id=1, source_target_pairs={{16,32},{48,64},{80,96},{32,16},{64,48},{96,80},{17,33},{49,65},{8... | collective-permute-start | bytes 516104 | tf_op jit(solution)/shard_map/ppermute | solution.py:571
  5.4 1.7 %collective-permute-start = (f32[48,128]{1,0:T(8,128)S(1)}, f32[48,128]{1,0:T(8,128)S(1)}, u32[]{:S(2)}, u32[]{:S(2)}) collective-permute-start(f32[48,128]{1,0:T(8,128)S(1)} %get-tuple-element.39), channel_id=1, source_target_pairs={{0,1},{1,0},{2,3},{3,2},{4,5},{5,4},{6,7},{7,6},{8,9},{9,8},{10,11... | collective-permute-start | bytes 73736 | tf_op jit(solution)/shard_map/ppermute | solution.py:572
  7.0 0.7 collective-permute-start.1
  7.7 0.0 copy-done
  7.8 1.8 %shard_map.149 = (f32[31,7,72,128]{3,2,1,0:T(8,128)S(1)}, f32[7,576,128]{2,1,0:T(8,128)S(1)}, s32[8,128]{1,0:T(8,128)S(1)}, s32[1,1]{1,0:T(1,128)}, f32[14,56,128]{2,1,0:T(8,128)S(1)}) custom-call(s32[8,128]{1,0:T(8,128)S(1)} %bitcast.6, f32[56,768]{1,0:T(8,128)S(1)} %get-tuple-element.37.refs_1_, f32[3,48,768]{2,1,0:T(8,128)S(1)} %copy-done, ...), custom_call_target="tpu_custom_call" | custom-call | flops 3000000 | bytes 6000000 | tf_op jit(solution)/shard_map/pallas_call | solution.py:539
  10.3 0.0 collective-permute-done.col_a
  10.3 0.0 collective-permute-done.1.col_b
  10.3 0.1 shard_map.150
  10.4 0.4 collective-permute-start.2
  10.8 2.4 %collective-permute-start.3 = (f32[8,128]{1,0:T(8,128)S(1)}, f32[8,128]{1,0:T(8,128)S(1)}, u32[]{:S(2)}, u32[]{:S(2)}) collective-permute-start(f32[8,128]{1,0:T(8,128)S(1)} %get-tuple-element.42), channel_id=1, source_target_pairs={{16,32},{48,64},{80,96},{32,16},{64,48},{96,80},{17,33},{49,65},{8... | collective-permute-start | bytes 12296 | tf_op jit(solution)/shard_map/ppermute | solution.py:571
  13.2 0.0 collective-permute-done.4.row_a
  13.2 0.0 collective-permute-done.5.row_b
  13.2 2.3 %shard_map.151 = (f32[31,7,72,128]{3,2,1,0:T(8,128)S(1)}, f32[7,576,128]{2,1,0:T(8,128)S(1)}, f32[14,56,128]{2,1,0:T(8,128)S(1)}, f32[16,112,128]{2,1,0:T(8,128)S(1)}) custom-call(f32[56,768]{1,0:T(8,128)S(1)} %collective-permute-done.4.row_a, ...), custom_call_target="tpu_custom_call", output_to_operand_aliasing={{0}: (3, {}), {1}: (4, {}), {2}: (5, {})} | custom-call | flops 3000000 | bytes 6000000 | tf_op jit(solution)/shard_map/pallas_call | solution.py:539
  15.5 0.0 collective-permute-done.2.cor_a
  15.5 0.2 collective-permute-done.3.cor_b
  15.7 0.9 %shard_map.152 = (f32[16,112,128]{2,1,0:T(8,128)S(1)}, f32[1,576,128]{2,1,0:T(8,128)S(1)}) custom-call(f32[48,128]{1,0:T(8,128)S(1)} %collective-permute-done.col_a, f32[48,128]{1,0:T(8,128)S(1)} %collective-permute-done.1.col_b, f32[8,128]{1,0:T(8,128)S(1)} %collective-permute-done.2.cor_a, ...), custom_call_target="tpu_custom_call", output_to_operand_aliasing={{0}: (6, {})} | custom-call | flops 2000000 | bytes 4000000 | tf_op jit(solution)/shard_map/pallas_call | solution.py:539
  16.6 48.8 %conditional.1 = ((f32[3,48,384]{2,1,0:T(8,128)}, f32[3,48,384]{2,1,0:T(8,128)}, f32[3,48,384]{2,1,0:T(8,128)}, f32[48,384]{1,0:T(8,128)}, f32[48,384]{1,0:T(8,128)}, /*index=5*/f32[48,384]{1,0:T(8,128)})) conditional(s32[]{:T(128)} %bitcast.3, (f32[16,112,128]{2,1,0:T(8,128)S(1)}, s32[8,128]{1,0:T(8,128)S(1)}) %tuple.13, (s32[8,128]{1,0:T(8,128)S(1)}, ...), branch_computations={%region_0.0_spmd, %region_1.0_spmd} | conditional | bytes 5505032 | solution.py:623
  16.7 27.7 %all_to_all.16 = f32[16,112,128]{2,1,0:T(8,128)S(1)} all-to-all(f32[16,112,128]{2,1,0:T(8,128)S(1)} %get-tuple-element.11), channel_id=1, replica_groups=mesh['gx'=8,'gy'=16] {'gy'}, dimensions={0} | all-to-all | bytes 1835008 | tf_op jit(solution)/shard_map/cond/branch_0_fun/all_to_all | solution.py:610
  44.4 1.4 %branch_0_fun.2 = f32[16,112,128]{2,1,0:T(8,128)S(1)} custom-call(s32[8,128]{1,0:T(8,128)S(1)} %get-tuple-element.10.idx, f32[1792,128]{1,0:T(8,128)S(1)} %bitcast.5), custom_call_target="tpu_custom_call" | custom-call | tf_op jit(solution)/shard_map/cond/branch_0_fun/pallas_call | solution.py:539
  45.8 18.7 %all_to_all.17.got = f32[16,112,128]{2,1,0:T(8,128)S(1)} all-to-all(f32[16,112,128]{2,1,0:T(8,128)S(1)} %branch_0_fun.2), channel_id=1, replica_groups=mesh['gx'=8,'gy'=16] {'gy'}, dimensions={0} | all-to-all | bytes 1835008 | tf_op jit(solution)/shard_map/cond/branch_0_fun/all_to_all | solution.py:613
  64.4 1.0 %branch_0_fun.3 = (f32[3,48,384]{2,1,0:T(8,128)}, f32[3,48,384]{2,1,0:T(8,128)}, f32[3,48,384]{2,1,0:T(8,128)}, f32[48,384]{1,0:T(8,128)}, f32[48,384]{1,0:T(8,128)}, /*index=5*/f32[48,384]{1,0:T(8,128)}) custom-call(s32[8,128]{1,0:T(8,128)S(1)} %get-tuple-element.10.idx, f32[16,112,128]{2,1,0:T(8,128)S(1)} %all_to_all.17.got), custom_call_target="tpu_custom_call" | custom-call | tf_op jit(solution)/shard_map/cond/branch_0_fun/pallas_call | solution.py:539
  (8 shorter events, 0.0 us)
Async XLA Ops:
  0.6 7.0 %copy-start = (f32[3,48,768]{2,1,0:T(8,128)S(1)}, f32[3,48,768]{2,1,0:T(8,128)}, u32[]{:S(2)}) copy-start(f32[3,48,768]{2,1,0:T(8,128)} %refs_2_.3) | copy-start | bytes 1327108
  0.6 7.0 %copy-start.1 = (f32[3,48,768]{2,1,0:T(8,128)S(1)}, f32[3,48,768]{2,1,0:T(8,128)}, u32[]{:S(2)}) copy-start(f32[3,48,768]{2,1,0:T(8,128)} %refs_3_.3) | copy-start | bytes 1327108
  0.7 7.0 %copy-start.2 = (f32[3,48,768]{2,1,0:T(8,128)S(1)}, f32[3,48,768]{2,1,0:T(8,128)}, u32[]{:S(2)}) copy-start(f32[3,48,768]{2,1,0:T(8,128)} %refs_4_.3) | copy-start | bytes 1327108
  0.7 7.0 %copy-start.3 = (f32[48,768]{1,0:T(8,128)S(1)}, f32[48,768]{1,0:T(8,128)}, u32[]{:S(2)}) copy-start(f32[48,768]{1,0:T(8,128)} %refs_5_.3) | copy-start | bytes 442372
  0.7 7.0 %copy-start.4 = (f32[48,768]{1,0:T(8,128)S(1)}, f32[48,768]{1,0:T(8,128)}, u32[]{:S(2)}) copy-start(f32[48,768]{1,0:T(8,128)} %refs_6_.3) | copy-start | bytes 442372
  0.7 7.0 %copy-start.5 = (f32[48,768]{1,0:T(8,128)S(1)}, f32[48,768]{1,0:T(8,128)}, u32[]{:S(2)}) copy-start(f32[48,768]{1,0:T(8,128)} %refs_7_.3) | copy-start | bytes 442372
  0.7 7.0 %copy-start.6 = (f32[48,768]{1,0:T(8,128)S(1)}, f32[48,768]{1,0:T(8,128)}, u32[]{:S(2)}) copy-start(f32[48,768]{1,0:T(8,128)} %refs_8_.1) | copy-start | bytes 442372
  0.7 7.0 %copy-start.7 = (s32[48,768]{1,0:T(8,128)S(1)}, s32[48,768]{1,0:T(8,128)}, u32[]{:S(2)}) copy-start(s32[48,768]{1,0:T(8,128)} %refs_9_.1) | copy-start | bytes 442372
  0.7 7.0 %copy-start.8 = (s32[1024]{0:T(1024)S(1)}, s32[1024]{0:T(1024)}, u32[]{:S(2)}) copy-start(s32[1024]{0:T(1024)} %param.19) | copy-start | bytes 12292
  2.7 10.4 %collective-permute-start.4 = (f32[56,768]{1,0:T(8,128)S(1)}, f32[56,768]{1,0:T(8,128)S(1)}, u32[]{:S(2)}, u32[]{:S(2)}) collective-permute-start(f32[56,768]{1,0:T(8,128)S(1)} %get-tuple-element.37.refs_1_), channel_id=1, source_target_pairs={{0,16},{16,0},{32,48},{48,32},{64,80},{80,64},{96,112},{112,96},{1... | collective-permute-start | bytes 516104 | tf_op jit(solution)/shard_map/ppermute | solution.py:572
  2.8 10.4 %collective-permute-start.5 = (f32[56,768]{1,0:T(8,128)S(1)}, f32[56,768]{1,0:T(8,128)S(1)}, u32[]{:S(2)}, u32[]{:S(2)}) collective-permute-start(f32[56,768]{1,0:T(8,128)S(1)} %get-tuple-element.44), channel_id=1, source_target_pairs={{16,32},{48,64},{80,96},{32,16},{64,48},{96,80},{17,33},{49,65},{8... | collective-permute-start | bytes 516104 | tf_op jit(solution)/shard_map/ppermute | solution.py:571
  5.4 4.9 %collective-permute-start = (f32[48,128]{1,0:T(8,128)S(1)}, f32[48,128]{1,0:T(8,128)S(1)}, u32[]{:S(2)}, u32[]{:S(2)}) collective-permute-start(f32[48,128]{1,0:T(8,128)S(1)} %get-tuple-element.39), channel_id=1, source_target_pairs={{0,1},{1,0},{2,3},{3,2},{4,5},{5,4},{6,7},{7,6},{8,9},{9,8},{10,11... | collective-permute-start | bytes 73736 | tf_op jit(solution)/shard_map/ppermute | solution.py:572
  7.0 3.3 %collective-permute-start.1 = (f32[48,128]{1,0:T(8,128)S(1)}, f32[48,128]{1,0:T(8,128)S(1)}, u32[]{:S(2)}, u32[]{:S(2)}) collective-permute-start(f32[48,128]{1,0:T(8,128)S(1)} %get-tuple-element.40), channel_id=1, source_target_pairs={{1,2},{3,4},{5,6},{7,8},{9,10},{11,12},{13,14},{2,1},{4,3},{6,5},{... | collective-permute-start | bytes 73736 | tf_op jit(solution)/shard_map/ppermute | solution.py:571
  10.4 5.1 %collective-permute-start.2 = (f32[8,128]{1,0:T(8,128)S(1)}, f32[8,128]{1,0:T(8,128)S(1)}, u32[]{:S(2)}, u32[]{:S(2)}) collective-permute-start(f32[8,128]{1,0:T(8,128)S(1)} %get-tuple-element.41), channel_id=1, source_target_pairs={{0,16},{16,0},{32,48},{48,32},{64,80},{80,64},{96,112},{112,96},{1... | collective-permute-start | bytes 12296 | tf_op jit(solution)/shard_map/ppermute | solution.py:572
  10.8 4.9 %collective-permute-start.3 = (f32[8,128]{1,0:T(8,128)S(1)}, f32[8,128]{1,0:T(8,128)S(1)}, u32[]{:S(2)}, u32[]{:S(2)}) collective-permute-start(f32[8,128]{1,0:T(8,128)S(1)} %get-tuple-element.42), channel_id=1, source_target_pairs={{16,32},{48,64},{80,96},{32,16},{64,48},{96,80},{17,33},{49,65},{8... | collective-permute-start | bytes 12296 | tf_op jit(solution)/shard_map/ppermute | solution.py:571
